TPU v7x, 32 devices: a whole 2x2x4 slice. The times are simulated.
32 devices in a mesh: row: 8 (over z, x), col: 4 (over y, core).
Axes of the slice: x: 2, y: 2, z: 4, core: 2. Of those that a mesh axis runs over, the one named last changes fastest.
Arguments:
- vertex: bfloat16 [64, 4096, 4096], P(None, 'row', 'col'), may hold values from -6 to 6
- a_factor: bfloat16 [4096, 1024], P('row', 'col'), as said below
- b_factor: bfloat16 [4096, 1024], P('col', 'row'), as said below
Outputs:
- field_factor: float32 [64, 1024], P(None, 'col')
Inputs may be any that keep to these rules, and one draw needn't show every extreme that they name: `a_factor`: entries lie within -12 / sqrt(4096) and 12 / sqrt(4096). `b_factor`: entries lie within -12 / sqrt(4096) and 12 / sqrt(4096).
All inputs are finite; a program needn't handle non-finite values.
Results may differ from a plain program's by a relative error of at most 0.0003.
Values may be sent and summed in bfloat16 or wider, within the bound.
No kernel may reach another device: no remote copies, remote signals or barrier semaphores. Data moves between devices by JAX's collectives and lax.ppermute only.
A program may use at most 128 MiB of HBM per device.

v0:
```python
import jax
import jax.numpy as jnp
from jax import lax
from jax.sharding import PartitionSpec as P

ridge_term = 0.25


def on_device(vertex, a_factor, b_factor):
    fields, p_local, q_local = vertex.shape
    rank_cols = a_factor.shape[1]
    row_rank = b_factor.shape[1]
    a_rows = lax.all_gather(a_factor, "col", axis=1, tiled=True)
    total_rank = a_rows.shape[1]
    groups = fields // 4
    stacked = vertex.reshape(groups, 4 * p_local, q_local)
    column_block = lax.all_gather(b_factor, "row", axis=1, tiled=True)
    width_now = column_block.shape[1]
    a_cols = a_rows.astype(jnp.float32)

    def one_group(slab):
        product = jnp.dot(slab, column_block, preferred_element_type=jnp.float32)
        product = product.reshape(4, p_local, width_now) * a_cols[None]
        return jnp.sum(product, axis=1)

    field_part = lax.map(one_group, stacked).reshape(fields, width_now)
    gram_part = lax.dot_general(
        b_factor, column_block, (((0,), (0,)), ((), ())), preferred_element_type=jnp.float32
    )
    joined = jnp.concatenate([field_part, gram_part], axis=0)
    m_part = joined[:fields]
    gb_part = joined[fields:]
    ga_part = lax.dot_general(
        a_factor, a_rows, (((0,), (0,)), ((), ())), preferred_element_type=jnp.float32
    )
    m_total = lax.psum(m_part, ("row", "col"))
    ga_tile = lax.psum_scatter(ga_part, "row", scatter_dimension=1, tiled=True)
    gb_tile = lax.psum_scatter(gb_part, "col", scatter_dimension=1, tiled=True)
    product_tile = ga_tile * gb_tile.T
    tiles = lax.all_gather(product_tile[None], ("row", "col"), axis=0, tiled=True)
    row_count = lax.axis_size("row")
    col_count = lax.axis_size("col")
    weight = (
        tiles.reshape(row_count, col_count, rank_cols, row_rank)
        .transpose(1, 2, 0, 3)
        .reshape(total_rank, total_rank)
    )
    weight = weight + ridge_term * jnp.eye(total_rank, dtype=jnp.float32)
    factor_lower = jnp.linalg.cholesky(weight)
    solved = jax.scipy.linalg.cho_solve((factor_lower, True), m_total.T)
    col_index = lax.axis_index("col")
    return lax.dynamic_slice_in_dim(solved.T, col_index * rank_cols, rank_cols, 1)


def solution(mesh):
    return jax.shard_map(
        on_device,
        mesh=mesh,
        in_specs=(P(None, "row", "col"), P("row", "col"), P("col", "row")),
        out_specs=P(None, "col"),
        check_vma=False,
    )
```

profile of v0, /device:TPU:0, one launch (start us, length us, event | category | flops | bytes accessed | tf_op | source)
XLA Modules:
  0.0 671.2 jit_solution(9382028890872371031)
XLA Ops:
  8.1 20.4 %all-gather.5.cloned.1.call-done = bf16[512,1024]{1,0:T(8,128)(2,1)} async-done(((bf16[512,256]{1,0:T(8,128)(2,1)}), bf16[512,1024]{1,0:T(8,128)(2,1)}) %all-gather.5.cloned.1.call-update) | async-done | bytes 1048592 | tf_op jit(solution)/shard_map/all_gather | solution.py:13
  31.5 50.2 %all-gather.7.cloned.1.call-done = bf16[1024,1024]{1,0:T(8,128)(2,1)} async-done(((bf16[1024,128]{1,0:T(8,128)(2,1)}), bf16[1024,1024]{1,0:T(8,128)(2,1)}) %all-gather.7.cloned.1.call-update) | async-done | bytes 2097168 | tf_op jit(solution)/shard_map/all_gather | solution.py:17
  85.4 61.8 %reduce-scatter.3.cloned.1.call-done = f32[256,128]{1,0:T(8,128)} async-done(((f32[256,1024]{1,0:T(8,128)}), f32[256,128]{1,0:T(8,128)}) %reduce-scatter.3.cloned.1.call-update) | async-done | bytes 131088 | tf_op jit(solution)/shard_map/reduce_scatter | solution.py:37
  147.2 23.2 %reduce-scatter.5.cloned.1.call-done = f32[128,256]{0,1:T(8,128)} async-done(((f32[128,1024]{0,1:T(8,128)}), f32[128,256]{0,1:T(8,128)}) %reduce-scatter.5.cloned.1.call-update) | async-done | bytes 131088 | tf_op jit(solution)/shard_map/reduce_scatter | solution.py:38
  172.1 123.0 %while.11 = (s32[]{:T(128)}, f32[16,4,1024]{2,1,0:T(4,128)S(1)}, bf16[16,2048,1024]{2,1,0:T(8,128)(2,1)}, bf16[1024,1024]{1,0:T(8,128)(2,1)}, f32[512,1024]{1,0:T(8,128)S(1)}, /*index=5*/s32[]{:T(128)}) while((s32[]{:T(128)}, f32[16,4,1024]{2,1,0:T(4,128)S(1)}, bf16[16,2048,1024]{2,1,0:T(8,128)(2,1)}, bf16[1024,1024]{1,0:T(8,128)(2,1)}, ...), condition=%wide.region_20.21_spmd, body=%wide.region_18.20_spmd.sunk | while | flops 4299157504 | bytes 25215088 | solution.py:26
  296.0 5.2 copy.5
  308.7 5.8 copy.6
  321.0 11.7 %cholesky.222 = f32[128,128]{1,0:T(8,128)S(1)} custom-call(f32[128,128]{1,0:T(8,128)S(1)} %cholesky.577), custom_call_target="Cholesky" | custom-call | tf_op jit(solution)/shard_map/jit(cholesky)/cholesky | solution.py:49
  332.8 9.8 %custom-call.66 = f32[1,128,128]{1,2,0:T(8,128)S(1)} custom-call(f32[1,128,128]{2,1,0:T(8,128)S(1)} %get-tuple-element.78), custom_call_target="InvertDiagBlocksLowerTriangular" | custom-call | tf_op jit(solution)/shard_map/jit(cholesky)/cholesky | solution.py:49
  346.0 11.7 %cholesky.243 = f32[128,128]{1,0:T(8,128)S(1)} custom-call(f32[128,128]{1,0:T(8,128)S(1)} %cholesky.581), custom_call_target="Cholesky" | custom-call | tf_op jit(solution)/shard_map/jit(cholesky)/cholesky | solution.py:49
  358.0 9.8 %custom-call.67 = f32[1,128,128]{1,2,0:T(8,128)S(1)} custom-call(f32[1,128,128]{2,1,0:T(8,128)S(1)} %get-tuple-element.76), custom_call_target="InvertDiagBlocksLowerTriangular" | custom-call | tf_op jit(solution)/shard_map/jit(cholesky)/cholesky | solution.py:49
  373.3 11.7 %cholesky.466 = f32[128,128]{1,0:T(8,128)S(1)} custom-call(f32[128,128]{1,0:T(8,128)S(1)} %cholesky.586), custom_call_target="Cholesky" | custom-call | tf_op jit(solution)/shard_map/jit(cholesky)/cholesky | solution.py:49
  385.8 9.8 %custom-call.68 = f32[1,128,128]{1,2,0:T(8,128)S(1)} custom-call(f32[1,128,128]{2,1,0:T(8,128)S(1)} %get-tuple-element.74), custom_call_target="InvertDiagBlocksLowerTriangular" | custom-call | tf_op jit(solution)/shard_map/jit(cholesky)/cholesky | solution.py:49
  400.2 11.7 %cholesky.485 = f32[128,128]{1,0:T(8,128)S(1)} custom-call(f32[128,128]{1,0:T(8,128)S(1)} %cholesky.591), custom_call_target="Cholesky" | custom-call | tf_op jit(solution)/shard_map/jit(cholesky)/cholesky | solution.py:49
  412.7 9.8 %custom-call.69 = f32[1,128,128]{1,2,0:T(8,128)S(1)} custom-call(f32[1,128,128]{2,1,0:T(8,128)S(1)} %get-tuple-element.72), custom_call_target="InvertDiagBlocksLowerTriangular" | custom-call | tf_op jit(solution)/shard_map/jit(cholesky)/cholesky | solution.py:49
  426.8 12.1 %cholesky.504 = f32[128,128]{1,0:T(8,128)S(1)} custom-call(f32[128,128]{1,0:T(8,128)S(1)} %cholesky.596), custom_call_target="Cholesky" | custom-call | tf_op jit(solution)/shard_map/jit(cholesky)/cholesky | solution.py:49
  439.7 9.8 %custom-call.70 = f32[1,128,128]{1,2,0:T(8,128)S(1)} custom-call(f32[1,128,128]{2,1,0:T(8,128)S(1)} %get-tuple-element.70), custom_call_target="InvertDiagBlocksLowerTriangular" | custom-call | tf_op jit(solution)/shard_map/jit(cholesky)/cholesky | solution.py:49
  453.7 11.7 %cholesky.524 = f32[128,128]{1,0:T(8,128)S(1)} custom-call(f32[128,128]{1,0:T(8,128)S(1)} %cholesky.601), custom_call_target="Cholesky" | custom-call | tf_op jit(solution)/shard_map/jit(cholesky)/cholesky | solution.py:49
  466.2 9.8 %custom-call.71 = f32[1,128,128]{1,2,0:T(8,128)S(1)} custom-call(f32[1,128,128]{2,1,0:T(8,128)S(1)} %get-tuple-element.68), custom_call_target="InvertDiagBlocksLowerTriangular" | custom-call | tf_op jit(solution)/shard_map/jit(cholesky)/cholesky | solution.py:49
  479.9 11.7 %cholesky.544 = f32[128,128]{1,0:T(8,128)S(1)} custom-call(f32[128,128]{1,0:T(8,128)S(1)} %cholesky.606), custom_call_target="Cholesky" | custom-call | tf_op jit(solution)/shard_map/jit(cholesky)/cholesky | solution.py:49
  492.4 9.8 %custom-call.72 = f32[1,128,128]{1,2,0:T(8,128)S(1)} custom-call(f32[1,128,128]{2,1,0:T(8,128)S(1)} %get-tuple-element.66), custom_call_target="InvertDiagBlocksLowerTriangular" | custom-call | tf_op jit(solution)/shard_map/jit(cholesky)/cholesky | solution.py:49
  505.2 11.7 %cholesky.562 = f32[128,128]{1,0:T(8,128)S(1)} custom-call(f32[128,128]{1,0:T(8,128)S(1)} %convolution_subtract_fusion.6), custom_call_target="Cholesky" | custom-call | tf_op jit(solution)/shard_map/jit(cholesky)/cholesky | solution.py:49
  532.1 28.6 %while.12 = (s32[]{:T(128)}, f32[1024,1024]{0,1:T(8,128)}, s32[8,2]{0,1:T(2,128)S(1)}, f32[8,128,128]{2,1,0:T(8,128)}, s32[]{:T(128)}) while((s32[]{:T(128)}, f32[1024,1024]{0,1:T(8,128)}, s32[8,2]{0,1:T(2,128)S(1)}, f32[8,128,128]{2,1,0:T(8,128)}, s32[]{:T(128)}) %tuple.65), condition=%wide.while_cond, body=%wide.while_body.sunk | while | flops 2 | bytes 393329 | solution.py:50
  560.7 79.6 %custom-call.73 = f32[8,128,128]{1,2,0:T(8,128)S(1)} custom-call(f32[8,128,128]{2,1,0:T(8,128)} %get-tuple-element.40), custom_call_target="InvertDiagBlocksLowerTriangular" | custom-call | tf_op jit(solution)/shard_map/jit(_cho_solve)/triangular_solve | solution.py:50
  (262 shorter events, 242.1 us)
Async XLA Ops:
  6.5 22.0 %all-gather.5.cloned.1.call-start = ((), (), s32[]{:S(2)}) async-start(), calls=%async_computation.2 | async-start | bytes 1310720 | tf_op jit(solution)/shard_map/all_gather | solution.py:13
  7.3 74.4 %all-gather.7.cloned.1.call-start = ((), (), s32[]{:S(2)}) async-start(), calls=%async_computation.4 | async-start | bytes 2359296 | tf_op jit(solution)/shard_map/all_gather | solution.py:17
  8.0 139.2 %reduce-scatter.3.cloned.1.call-start = ((), (), s32[]{:S(2)}) async-start(), calls=%async_computation.3 | async-start | bytes 1179648 | tf_op jit(solution)/shard_map/reduce_scatter | solution.py:37
  28.5 56.7 %copy-start.3 = (bf16[512,1024]{1,0:T(8,128)(2,1)S(1)}, bf16[512,1024]{1,0:T(8,128)(2,1)}, u32[]{:S(2)}) copy-start(bf16[512,1024]{1,0:T(8,128)(2,1)} %all-gather.5.cloned.1.call-done) | copy-start | bytes 3145732
  31.4 139.0 %reduce-scatter.5.cloned.1.call-start = ((), (), s32[]{:S(2)}) async-start(), calls=%async_computation.5 | async-start | bytes 655360 | tf_op jit(solution)/shard_map/reduce_scatter | solution.py:38
  85.1 210.9 %all-gather.9.cloned.1.call-start = ((), (), s32[]{:S(2)}) async-start(), calls=%async_computation.7 | async-start | bytes 4325376 | tf_op jit(solution)/shard_map/all_gather | solution.py:40
  172.0 468.3 %all-reduce.3.cloned.1.call-start = ((), (), s32[]{:S(2)}) async-start(), calls=%async_computation.6 | async-start | bytes 524288 | tf_op jit(solution)/shard_map/psum | solution.py:36
  172.1 2.9 copy-start.4
  179.8 3.0 copy-start.4
  187.6 2.9 copy-start.4
  195.2 2.9 copy-start.4
  202.9 2.9 copy-start.4
  210.6 2.9 copy-start.4
  218.3 2.9 copy-start.4
  226.0 2.9 copy-start.4
  233.7 2.9 copy-start.4
  241.4 2.9 copy-start.4
  249.1 2.9 copy-start.4
  256.8 2.9 copy-start.4
  264.5 2.9 copy-start.4
  272.1 2.9 copy-start.4
  279.8 2.9 copy-start.4
  287.5 2.9 copy-start.4
  368.9 2.0 copy-start
  (2 other events, 3.9 us)
Sparse Core Ops, SparseCore 0:
  8.9 19.5 all-gather.4
  30.5 51.0 all-gather.6
  85.0 62.1 reduce-scatter.2
  149.7 20.6 reduce-scatter.4
  173.1 62.0 all-gather.8
  296.1 125.8 all-reduce.2
where the time goes:
time: 678 us; the launch traced here: 671 us
  other arithmetic  261 us (38%)
  waiting for transfers between devices  157 us (23%)
  matrix products  131 us (19%)
  local copies, waits for them, and re-layouts  102 us (15%)
  between operations  19.4 us (3%)
    another operation x30, other arithmetic, on_device(): factor_lower = jnp.linalg.cholesky(weight)  168 us
    another operation x3, other arithmetic, on_device(): solved = jax.scipy.linalg.cho_solve((factor_lower, True), m_total.T)  84.4 us
    dot_general x16, matrix products, one_group(): product = jnp.dot(slab, column_block, preferred_element_type=jnp.float32)  76.5 us
    reduce_scatter x1, waiting for transfers between devices, on_device(): ga_tile = lax.psum_scatter(ga_part, 'row', scatter_dimension=1, tiled=True)  61.8 us
    all_gather x1, waiting for transfers between devices, on_device(): column_block = lax.all_gather(b_factor, 'row', axis=1, tiled=True)  50.2 us
    dynamic_slice x16, local copies, waits for them, and re-layouts, on_device(): field_part = lax.map(one_group, stacked).reshape(fields, width_now)  44.7 us
    another operation x40, local copies, waits for them, and re-layouts  28.5 us
    another operation x14, matrix products, on_device(): factor_lower = jnp.linalg.cholesky(weight)  25.9 us
  transfers between devices with their start and end apart: 6, of which 4 were waited for; matrix products, arithmetic and copies ran while one was open for 69% of the time, Pallas kernels for 0%

commit v1 on v0

--- a/solution.py
+++ b/solution.py
@@ -14,7 +14,20 @@
     total_rank = a_rows.shape[1]
     groups = fields // 4
     stacked = vertex.reshape(groups, 4 * p_local, q_local)
-    column_block = lax.all_gather(b_factor, "row", axis=1, tiled=True)
+    n_dev_all = lax.axis_size("row")
+    steps_seen = [(t, (t + 1) % n_dev_all) for t in range(n_dev_all)]
+    column = [(t, (t - 1) % n_dev_all) for t in range(n_dev_all)]
+    last, h_now = ([b_factor], [b_factor])
+    for _ in range(n_dev_all // 2):
+        last.append(lax.ppermute(last[-1], "row", steps_seen))
+    for _ in range((n_dev_all - 1) // 2):
+        back = lax.ppermute(h_now[-1], "row", column)
+        h_now.append(back)
+    column_block = jnp.roll(
+        jnp.concatenate([*last[::-1], *h_now[1:]], axis=1),
+        (lax.axis_index("row") - n_dev_all // 2) * b_factor.shape[1],
+        axis=1,
+    )
     width_now = column_block.shape[1]
     a_cols = a_rows.astype(jnp.float32)
 

time: 678 us -> 654 us (0.965)
  waiting for transfers between devices: 157 us -> 109 us
  starting transfers between devices: 0.2 us -> 27.2 us
    all_gather x1 -> x0, waiting for transfers between devices: 50.2 us -> none  [on_device(): column_block = lax.all_gather(b_factor, 'row', axis=1, tiled=True)]
    ppermute x0 -> x7, starting transfers between devices: none -> 27.1 us  [the longest x3 19.2 us: on_device(): back = lax.ppermute(h_now[-1], 'row', column)]
    ppermute x0 -> x7, waiting for transfers between devices: none -> 22.7 us  [the longest x4 21.6 us: on_device(): last.append(lax.ppermute(last[-1], 'row', steps_seen))]
    all_gather x1, waiting for transfers between devices: 20.4 us -> 0.02 us  [on_device(): a_rows = lax.all_gather(a_factor, 'col', axis=1, tiled=True)]
  transfers between devices with their start and end apart: 6 -> 12, of which waited for: 4 -> 7; matrix products, arithmetic and copies ran while one was open for 69% -> 71% of each run, Pallas kernels for 0% -> 0%
where the time goes in v1:
time: 654 us; the launch traced here: 646 us
  other arithmetic  263 us (40%)
  matrix products  128 us (20%)
  waiting for transfers between devices  109 us (17%)
  local copies, waits for them, and re-layouts  99.4 us (15%)
  starting transfers between devices  27.2 us (4%)
  between operations  19.2 us (3%)
    another operation x30, other arithmetic, on_device(): factor_lower = jnp.linalg.cholesky(weight)  168 us
    another operation x3, other arithmetic, on_device(): solved = jax.scipy.linalg.cho_solve((factor_lower, True), m_total.T)  83.6 us
    dot_general x16, matrix products, one_group(): product = jnp.dot(slab, column_block, preferred_element_type=jnp.float32)  75.4 us
    reduce_scatter x1, waiting for transfers between devices, on_device(): ga_tile = lax.psum_scatter(ga_part, 'row', scatter_dimension=1, tiled=True)  67.7 us
    dynamic_slice x16, local copies, waits for them, and re-layouts, on_device(): field_part = lax.map(one_group, stacked).reshape(fields, width_now)  44.7 us
    another operation x14, matrix products, on_device(): factor_lower = jnp.linalg.cholesky(weight)  25.9 us
    another operation x40, local copies, waits for them, and re-layouts  23.6 us
    another operation x30, matrix products, on_device(): solved = jax.scipy.linalg.cho_solve((factor_lower, True), m_total.T)  22.6 us
  transfers between devices with their start and end apart: 12, of which 7 were waited for; matrix products, arithmetic and copies ran while one was open for 71% of the time, Pallas kernels for 0%

profile of v1, /device:TPU:0, one launch (start us, length us, event | category | flops | bytes accessed | tf_op | source)
XLA Modules:
  0.0 646.4 jit_solution(7048370617202390126)
XLA Ops:
  9.5 9.6 %collective-permute-done = bf16[1024,128]{1,0:T(8,128)(2,1)S(1)} collective-permute-done((bf16[1024,128]{1,0:T(8,128)(2,1)}, bf16[1024,128]{1,0:T(8,128)(2,1)S(1)}, u32[]{:S(2)}, u32[]{:S(2)}) %collective-permute-start) | collective-permute-done | bytes 262176 | tf_op jit(solution)/shard_map/ppermute | solution.py:22
  23.8 6.2 collective-permute-done.1
  32.5 6.6 %collective-permute-start.5 = (bf16[1024,128]{1,0:T(8,128)(2,1)S(1)}, bf16[1024,128]{1,0:T(8,128)(2,1)S(1)}, u32[]{:S(2)}, u32[]{:S(2)}) collective-permute-start(bf16[1024,128]{1,0:T(8,128)(2,1)S(1)} %collective-permute-done.4), channel_id=1, source_target_pairs={{0,28},{4,0},{8,4},{12,8},{16,12},{20,16},{24,20},{28,24},{1,29},{... | collective-permute-start | bytes 786440 | tf_op jit(solution)/shard_map/ppermute | solution.py:24
  45.1 7.8 %collective-permute-start.6 = (bf16[1024,128]{1,0:T(8,128)(2,1)S(1)}, bf16[1024,128]{1,0:T(8,128)(2,1)S(1)}, u32[]{:S(2)}, u32[]{:S(2)}) collective-permute-start(bf16[1024,128]{1,0:T(8,128)(2,1)S(1)} %collective-permute-done.5), channel_id=1, source_target_pairs={{0,28},{4,0},{8,4},{12,8},{16,12},{20,16},{24,20},{28,24},{1,29},{... | collective-permute-start | bytes 786440 | tf_op jit(solution)/shard_map/ppermute | solution.py:24
  66.4 18.5 %reduce-scatter.5.cloned.1.call-done = f32[128,256]{0,1:T(8,128)} async-done(((f32[128,1024]{0,1:T(8,128)}), f32[128,256]{0,1:T(8,128)}) %reduce-scatter.5.cloned.1.call-update) | async-done | bytes 131088 | tf_op jit(solution)/shard_map/reduce_scatter | solution.py:51
  84.8 67.7 %reduce-scatter.3.cloned.1.call-done = f32[256,128]{1,0:T(8,128)} async-done(((f32[256,1024]{1,0:T(8,128)}), f32[256,128]{1,0:T(8,128)}) %reduce-scatter.3.cloned.1.call-update) | async-done | bytes 131088 | tf_op jit(solution)/shard_map/reduce_scatter | solution.py:50
  154.2 122.0 %while.11 = (s32[]{:T(128)}, f32[16,4,1024]{2,1,0:T(4,128)S(1)}, bf16[16,2048,1024]{2,1,0:T(8,128)(2,1)}, bf16[1024,1024]{1,0:T(8,128)(2,1)S(1)}, f32[512,1024]{1,0:T(8,128)}, /*index=5*/s32[]{:T(128)}) while((s32[]{:T(128)}, f32[16,4,1024]{2,1,0:T(4,128)S(1)}, bf16[16,2048,1024]{2,1,0:T(8,128)(2,1)}, bf16[1024,1024]{1,0:T(8,128)(2,1)S(1)}, ...), condition=%wide.region_20.21_spmd, body=%wide.region_18.20_spmd.sunk | while | flops 4299157504 | bytes 25215088 | solution.py:39
  302.1 11.7 %cholesky.222 = f32[128,128]{1,0:T(8,128)S(1)} custom-call(f32[128,128]{1,0:T(8,128)S(1)} %cholesky.577), custom_call_target="Cholesky" | custom-call | tf_op jit(solution)/shard_map/jit(cholesky)/cholesky | solution.py:62
  313.9 9.8 %custom-call.66 = f32[1,128,128]{1,2,0:T(8,128)S(1)} custom-call(f32[1,128,128]{2,1,0:T(8,128)S(1)} %get-tuple-element.78), custom_call_target="InvertDiagBlocksLowerTriangular" | custom-call | tf_op jit(solution)/shard_map/jit(cholesky)/cholesky | solution.py:62
  327.1 11.7 %cholesky.243 = f32[128,128]{1,0:T(8,128)S(1)} custom-call(f32[128,128]{1,0:T(8,128)S(1)} %cholesky.581), custom_call_target="Cholesky" | custom-call | tf_op jit(solution)/shard_map/jit(cholesky)/cholesky | solution.py:62
  339.1 9.8 %custom-call.67 = f32[1,128,128]{1,2,0:T(8,128)S(1)} custom-call(f32[1,128,128]{2,1,0:T(8,128)S(1)} %get-tuple-element.76), custom_call_target="InvertDiagBlocksLowerTriangular" | custom-call | tf_op jit(solution)/shard_map/jit(cholesky)/cholesky | solution.py:62
  354.4 11.7 %cholesky.466 = f32[128,128]{1,0:T(8,128)S(1)} custom-call(f32[128,128]{1,0:T(8,128)S(1)} %cholesky.586), custom_call_target="Cholesky" | custom-call | tf_op jit(solution)/shard_map/jit(cholesky)/cholesky | solution.py:62
  366.9 9.8 %custom-call.68 = f32[1,128,128]{1,2,0:T(8,128)S(1)} custom-call(f32[1,128,128]{2,1,0:T(8,128)S(1)} %get-tuple-element.74), custom_call_target="InvertDiagBlocksLowerTriangular" | custom-call | tf_op jit(solution)/shard_map/jit(cholesky)/cholesky | solution.py:62
  381.3 11.7 %cholesky.485 = f32[128,128]{1,0:T(8,128)S(1)} custom-call(f32[128,128]{1,0:T(8,128)S(1)} %cholesky.591), custom_call_target="Cholesky" | custom-call | tf_op jit(solution)/shard_map/jit(cholesky)/cholesky | solution.py:62
  393.8 9.8 %custom-call.69 = f32[1,128,128]{1,2,0:T(8,128)S(1)} custom-call(f32[1,128,128]{2,1,0:T(8,128)S(1)} %get-tuple-element.72), custom_call_target="InvertDiagBlocksLowerTriangular" | custom-call | tf_op jit(solution)/shard_map/jit(cholesky)/cholesky | solution.py:62
  407.9 12.1 %cholesky.504 = f32[128,128]{1,0:T(8,128)S(1)} custom-call(f32[128,128]{1,0:T(8,128)S(1)} %cholesky.596), custom_call_target="Cholesky" | custom-call | tf_op jit(solution)/shard_map/jit(cholesky)/cholesky | solution.py:62
  420.8 9.8 %custom-call.70 = f32[1,128,128]{1,2,0:T(8,128)S(1)} custom-call(f32[1,128,128]{2,1,0:T(8,128)S(1)} %get-tuple-element.70), custom_call_target="InvertDiagBlocksLowerTriangular" | custom-call | tf_op jit(solution)/shard_map/jit(cholesky)/cholesky | solution.py:62
  434.8 11.7 %cholesky.524 = f32[128,128]{1,0:T(8,128)S(1)} custom-call(f32[128,128]{1,0:T(8,128)S(1)} %cholesky.601), custom_call_target="Cholesky" | custom-call | tf_op jit(solution)/shard_map/jit(cholesky)/cholesky | solution.py:62
  447.3 9.8 %custom-call.71 = f32[1,128,128]{1,2,0:T(8,128)S(1)} custom-call(f32[1,128,128]{2,1,0:T(8,128)S(1)} %get-tuple-element.68), custom_call_target="InvertDiagBlocksLowerTriangular" | custom-call | tf_op jit(solution)/shard_map/jit(cholesky)/cholesky | solution.py:62
  461.0 11.7 %cholesky.544 = f32[128,128]{1,0:T(8,128)S(1)} custom-call(f32[128,128]{1,0:T(8,128)S(1)} %cholesky.606), custom_call_target="Cholesky" | custom-call | tf_op jit(solution)/shard_map/jit(cholesky)/cholesky | solution.py:62
  473.5 9.8 %custom-call.72 = f32[1,128,128]{1,2,0:T(8,128)S(1)} custom-call(f32[1,128,128]{2,1,0:T(8,128)S(1)} %get-tuple-element.66), custom_call_target="InvertDiagBlocksLowerTriangular" | custom-call | tf_op jit(solution)/shard_map/jit(cholesky)/cholesky | solution.py:62
  486.3 11.7 %cholesky.562 = f32[128,128]{1,0:T(8,128)S(1)} custom-call(f32[128,128]{1,0:T(8,128)S(1)} %convolution_subtract_fusion.6), custom_call_target="Cholesky" | custom-call | tf_op jit(solution)/shard_map/jit(cholesky)/cholesky | solution.py:62
  513.2 23.9 %while.12 = (s32[]{:T(128)}, f32[1024,1024]{0,1:T(8,128)}, s32[8,2]{0,1:T(2,128)S(1)}, f32[8,128,128]{2,1,0:T(8,128)S(1)}, s32[]{:T(128)}) while((s32[]{:T(128)}, f32[1024,1024]{0,1:T(8,128)}, s32[8,2]{0,1:T(2,128)S(1)}, f32[8,128,128]{2,1,0:T(8,128)S(1)}, s32[]{:T(128)}) %tuple.65), condition=%wide.while_cond, body=%wide.while_body.sunk | while | flops 2 | bytes 393329 | solution.py:63
  537.1 78.8 %custom-call.73 = f32[8,128,128]{1,2,0:T(8,128)S(1)} custom-call(f32[8,128,128]{2,1,0:T(8,128)S(1)} %get-tuple-element.40), custom_call_target="InvertDiagBlocksLowerTriangular" | custom-call | tf_op jit(solution)/shard_map/jit(_cho_solve)/triangular_solve | solution.py:63
  (292 shorter events, 268.4 us)
Async XLA Ops:
  6.5 51.9 %copy-start.3 = (bf16[1024,128]{1,0:T(8,128)(2,1)S(1)}, bf16[1024,128]{1,0:T(8,128)(2,1)}, u32[]{:S(2)}) copy-start(bf16[1024,128]{1,0:T(8,128)(2,1)} %param.7) | copy-start | bytes 786436
  6.5 54.2 %all-gather.4.cloned.1.call-start = ((), (), s32[]{:S(2)}) async-start(), calls=%async_computation.2 | async-start | bytes 1310720 | tf_op jit(solution)/shard_map/all_gather | solution.py:13
  6.5 12.6 %collective-permute-start = (bf16[1024,128]{1,0:T(8,128)(2,1)}, bf16[1024,128]{1,0:T(8,128)(2,1)S(1)}, u32[]{:S(2)}, u32[]{:S(2)}) collective-permute-start(bf16[1024,128]{1,0:T(8,128)(2,1)} %param.7), channel_id=1, source_target_pairs={{0,4},{4,8},{8,12},{12,16},{16,20},{20,24},{24,28},{28,0},{1,5},{5... | collective-permute-start | bytes 786440 | tf_op jit(solution)/shard_map/ppermute | solution.py:22
  19.1 10.9 %collective-permute-start.1 = (bf16[1024,128]{1,0:T(8,128)(2,1)S(1)}, bf16[1024,128]{1,0:T(8,128)(2,1)S(1)}, u32[]{:S(2)}, u32[]{:S(2)}) collective-permute-start(bf16[1024,128]{1,0:T(8,128)(2,1)S(1)} %collective-permute-done), channel_id=1, source_target_pairs={{0,4},{4,8},{8,12},{12,16},{16,20},{20,24},{24,28},{28,0},{1,5},{5... | collective-permute-start | bytes 786440 | tf_op jit(solution)/shard_map/ppermute | solution.py:22
  19.1 13.4 %collective-permute-start.4 = (bf16[1024,128]{1,0:T(8,128)(2,1)}, bf16[1024,128]{1,0:T(8,128)(2,1)S(1)}, u32[]{:S(2)}, u32[]{:S(2)}) collective-permute-start(bf16[1024,128]{1,0:T(8,128)(2,1)} %param.7), channel_id=1, source_target_pairs={{0,28},{4,0},{8,4},{12,8},{16,12},{20,16},{24,20},{28,24},{1,29},{... | collective-permute-start | bytes 786440 | tf_op jit(solution)/shard_map/ppermute | solution.py:24
  30.0 12.5 %collective-permute-start.2 = (bf16[1024,128]{1,0:T(8,128)(2,1)S(1)}, bf16[1024,128]{1,0:T(8,128)(2,1)S(1)}, u32[]{:S(2)}, u32[]{:S(2)}) collective-permute-start(bf16[1024,128]{1,0:T(8,128)(2,1)S(1)} %collective-permute-done.1), channel_id=1, source_target_pairs={{0,4},{4,8},{8,12},{12,16},{16,20},{20,24},{24,28},{28,0},{1,5},{5... | collective-permute-start | bytes 786440 | tf_op jit(solution)/shard_map/ppermute | solution.py:22
  32.5 12.6 %collective-permute-start.5 = (bf16[1024,128]{1,0:T(8,128)(2,1)S(1)}, bf16[1024,128]{1,0:T(8,128)(2,1)S(1)}, u32[]{:S(2)}, u32[]{:S(2)}) collective-permute-start(bf16[1024,128]{1,0:T(8,128)(2,1)S(1)} %collective-permute-done.4), channel_id=1, source_target_pairs={{0,28},{4,0},{8,4},{12,8},{16,12},{20,16},{24,20},{28,24},{1,29},{... | collective-permute-start | bytes 786440 | tf_op jit(solution)/shard_map/ppermute | solution.py:24
  42.5 12.8 %collective-permute-start.3 = (bf16[1024,128]{1,0:T(8,128)(2,1)S(1)}, bf16[1024,128]{1,0:T(8,128)(2,1)S(1)}, u32[]{:S(2)}, u32[]{:S(2)}) collective-permute-start(bf16[1024,128]{1,0:T(8,128)(2,1)S(1)} %collective-permute-done.2), channel_id=1, source_target_pairs={{0,4},{4,8},{8,12},{12,16},{16,20},{20,24},{24,28},{28,0},{1,5},{5... | collective-permute-start | bytes 786440 | tf_op jit(solution)/shard_map/ppermute | solution.py:22
  45.0 39.8 %reduce-scatter.5.cloned.1.call-start = ((), (), s32[]{:S(2)}) async-start(), calls=%async_computation.4 | async-start | bytes 655360 | tf_op jit(solution)/shard_map/reduce_scatter | solution.py:51
  45.1 12.9 %collective-permute-start.6 = (bf16[1024,128]{1,0:T(8,128)(2,1)S(1)}, bf16[1024,128]{1,0:T(8,128)(2,1)S(1)}, u32[]{:S(2)}, u32[]{:S(2)}) collective-permute-start(bf16[1024,128]{1,0:T(8,128)(2,1)S(1)} %collective-permute-done.5), channel_id=1, source_target_pairs={{0,28},{4,0},{8,4},{12,8},{16,12},{20,16},{24,20},{28,24},{1,29},{... | collective-permute-start | bytes 786440 | tf_op jit(solution)/shard_map/ppermute | solution.py:24
  60.7 91.9 %reduce-scatter.3.cloned.1.call-start = ((), (), s32[]{:S(2)}) async-start(), calls=%async_computation.3 | async-start | bytes 1179648 | tf_op jit(solution)/shard_map/reduce_scatter | solution.py:50
  63.5 213.6 %all-gather.6.cloned.1.call-start = ((), (), s32[]{:S(2)}) async-start(), calls=%async_computation.6 | async-start | bytes 4325376 | tf_op jit(solution)/shard_map/all_gather | solution.py:53
  154.2 461.8 %all-reduce.3.cloned.1.call-start = ((), (), s32[]{:S(2)}) async-start(), calls=%async_computation.5 | async-start | bytes 524288 | tf_op jit(solution)/shard_map/psum | solution.py:49
  161.9 2.9 copy-start.4
  169.5 2.9 copy-start.4
  177.2 3.0 copy-start.4
  184.9 2.9 copy-start.4
  192.5 2.9 copy-start.4
  200.1 2.9 copy-start.4
  207.7 2.9 copy-start.4
  215.4 2.9 copy-start.4
  223.0 2.9 copy-start.4
  230.6 2.9 copy-start.4
  238.2 2.9 copy-start.4
  (9 other events, 22.0 us)
Sparse Core Ops, SparseCore 0:
  45.1 15.5 all-gather.3
  63.2 21.6 reduce-scatter.4
  88.6 63.8 reduce-scatter.2
  155.3 61.0 all-gather.5
  277.2 124.6 all-reduce.2
